TPU v7x, 32 devices: a whole 2x2x4 slice. The times are simulated.
32 devices in a mesh: dp: 8 (over z, x), tensor: 4 (over y, core).
Axes of the slice: x: 2, y: 2, z: 4, core: 2. Of those that a mesh axis runs over, the one named last changes fastest.
Arguments:
- tokens: bfloat16 [48, 260, 768], P('dp'), may hold values from -6 to 6
- cotangent: bfloat16 [48, 260, 768], P('dp'), may hold values from -6 to 6
- split_point: int32 [48], P('dp'), may hold values from 0 to 32
- w_qkv: bfloat16 [3, 768, 768], P(None, None, 'tensor'), may hold values from -0.21875 to 0.21875
- w_out: bfloat16 [768, 768], P('tensor'), may hold values from -0.75 to 0.75
- w_up: bfloat16 [768, 3072], P(None, 'tensor'), may hold values from -0.21875 to 0.21875
- w_down: bfloat16 [3072, 768], P('tensor'), may hold values from -0.109375 to 0.109375
- gain_one: float32 [768], replicated, may hold values from 0.1 to 1.9
- shift_one: float32 [768], replicated, may hold values from -3 to 3
- gain_two: float32 [768], replicated, may hold values from 0.1 to 1.9
- shift_two: float32 [768], replicated, may hold values from -3 to 3
Outputs:
- output: bfloat16 [48, 260, 768], P('dp')
- grad_tokens: bfloat16 [48, 260, 768], P('dp')
- grad_qkv: float32 [3, 768, 768], P(None, 'dp', 'tensor')
- grad_out: float32 [768, 768], P('tensor', 'dp')
- grad_up: float32 [768, 3072], P('dp', 'tensor')
- grad_down: float32 [3072, 768], P('tensor', 'dp')
- grad_gain_one: float32 [768], P('dp')
- grad_shift_one: float32 [768], P('dp')
- grad_gain_two: float32 [768], P('dp')
- grad_shift_two: float32 [768], P('dp')
All inputs are finite; a program needn't handle non-finite values.
Results may differ from a plain program's by a relative error of at most 0.013.
Values sent between devices are 32-bit elements; how exact they have to be, the bound alone decides.
A program may use at most 128 MiB of HBM per device.

v0:
```python
from functools import partial
import jax
import jax.numpy as jnp
from jax import lax
from jax.sharding import PartitionSpec as P

HD = 64
PATCHES = 196
EPSILON = 1e-05


def layer_norm(values, gain_vec, shift_vec):
    row_mean = jnp.mean(values, axis=-1, keepdims=True)
    centered = values - row_mean
    variance = jnp.mean(centered * centered, axis=-1, keepdims=True)
    return centered * lax.rsqrt(variance + EPSILON) * gain_vec + shift_vec


def attention_forward(inputs, allowed, w_qkv, w_out, gain_one, shift_one):
    batch, length, width = inputs.shape
    local = w_qkv.shape[2]
    head_count = local // HD
    normed = layer_norm(inputs, gain_one, shift_one).astype(jnp.bfloat16)
    packed = jnp.einsum("btd,cde->cbte", normed, w_qkv, preferred_element_type=jnp.float32).astype(
        jnp.bfloat16
    )
    queries = packed[0].reshape(batch, length, head_count, HD)
    keys = packed[1].reshape(batch, length, head_count, HD)
    values = packed[2].reshape(batch, length, head_count, HD)
    scores = jnp.einsum(
        "bqhe,bkhe->bhqk", queries, keys, preferred_element_type=jnp.float32
    ) * HD ** (-0.5)
    scores = jnp.where(allowed[:, None], scores, -1e30)
    log_total = jax.nn.logsumexp(scores, axis=-1, keepdims=True)
    attn_probs = jnp.exp(scores - log_total)
    probs_low = attn_probs.astype(jnp.bfloat16)
    mixed = jnp.einsum("bhqk,bkhe->bqhe", probs_low, values, preferred_element_type=jnp.float32)
    mixed = mixed.reshape(batch, length, local).astype(jnp.bfloat16)
    partial_out = jnp.einsum("btk,kd->btd", mixed, w_out, preferred_element_type=jnp.float32)
    return (normed, queries, keys, values, attn_probs, probs_low, mixed, partial_out)


def mlp_forward(middle, w_up, gain_two, shift_two):
    normed_two = layer_norm(middle, gain_two, shift_two).astype(jnp.bfloat16)
    pre_act = jnp.einsum("btd,df->btf", normed_two, w_up, preferred_element_type=jnp.float32)
    activated = jax.nn.gelu(pre_act, approximate=False).astype(jnp.bfloat16)
    return (normed_two, pre_act, activated)


def per_device(
    tokens,
    cotangent,
    split_point,
    w_qkv,
    w_out,
    w_up,
    w_down,
    gain_one,
    shift_one,
    gain_two,
    shift_two,
):
    inputs = tokens.astype(jnp.float32)
    batch, length, width = tokens.shape
    local = w_qkv.shape[2]
    head_count = local // HD
    score_scale = HD ** (-0.5)
    places = jnp.arange(length, dtype=jnp.int32)
    limit = jnp.maximum(places[None, :, None], PATCHES + split_point[:, None, None] - 1)
    allowed = places[None, None, :] <= limit
    normed, queries, keys, values, attn_probs, probs_low, mixed, partial_out = attention_forward(
        inputs, allowed, w_qkv, w_out, gain_one, shift_one
    )
    middle = inputs + lax.psum(partial_out, "tensor")
    normed_two, pre_act, activated = mlp_forward(middle, w_up, gain_two, shift_two)
    branch = jnp.einsum("btf,fd->btd", activated, w_down, preferred_element_type=jnp.float32)
    output = (middle + lax.psum(branch, "tensor")).astype(jnp.bfloat16)
    normed, queries, keys, values, attn_probs, probs_low, mixed, partial_out = attention_forward(
        inputs, allowed, w_qkv, w_out, gain_one, shift_one
    )
    middle = inputs + lax.psum(partial_out, "tensor")
    normed_two, pre_act, activated = mlp_forward(middle, w_up, gain_two, shift_two)
    grad_output = cotangent.astype(jnp.float32)
    grad_act = jnp.einsum("btd,fd->btf", cotangent, w_down, preferred_element_type=jnp.float32)
    gelu_pull = jax.vjp(partial(jax.nn.gelu, approximate=False), pre_act)[1]
    grad_pre = gelu_pull(grad_act)[0].astype(jnp.bfloat16)
    grad_down_local = jnp.einsum(
        "btf,btd->fd", activated, cotangent, preferred_element_type=jnp.float32
    )
    grad_up_local = jnp.einsum(
        "btd,btf->df", normed_two, grad_pre, preferred_element_type=jnp.float32
    )
    grad_normed_two = lax.psum(
        jnp.einsum("btf,df->btd", grad_pre, w_up, preferred_element_type=jnp.float32), "tensor"
    )
    norm_two_pull = jax.vjp(layer_norm, middle, gain_two, shift_two)[1]
    grad_mid_norm, grad_gain_two, grad_shift_two = norm_two_pull(grad_normed_two)
    grad_middle = grad_output + grad_mid_norm
    grad_mid_low = grad_middle.astype(jnp.bfloat16)
    grad_out_local = jnp.einsum(
        "btk,btd->kd", mixed, grad_mid_low, preferred_element_type=jnp.float32
    )
    grad_mix = jnp.einsum("btd,kd->btk", grad_mid_low, w_out, preferred_element_type=jnp.float32)
    grad_mix = grad_mix.astype(jnp.bfloat16).reshape(batch, length, head_count, HD)
    grad_probs = jnp.einsum("bqhe,bkhe->bhqk", grad_mix, values, preferred_element_type=jnp.float32)
    row_terms = jnp.sum(attn_probs * grad_probs, axis=-1, keepdims=True)
    grad_scores = (attn_probs * (grad_probs - row_terms)).astype(jnp.bfloat16)
    grad_query = (
        jnp.einsum("bhqk,bkhe->bqhe", grad_scores, keys, preferred_element_type=jnp.float32)
        * score_scale
    )
    grad_key = (
        jnp.einsum("bhqk,bqhe->bkhe", grad_scores, queries, preferred_element_type=jnp.float32)
        * score_scale
    )
    grad_value = jnp.einsum(
        "bhqk,bqhe->bkhe", probs_low, grad_mix, preferred_element_type=jnp.float32
    )
    grad_packed = (
        jnp.stack([grad_query, grad_key, grad_value])
        .reshape(3, batch, length, local)
        .astype(jnp.bfloat16)
    )
    grad_qkv_local = jnp.einsum(
        "btd,cbte->cde", normed, grad_packed, preferred_element_type=jnp.float32
    )
    grad_normed = lax.psum(
        jnp.einsum("cbte,cde->btd", grad_packed, w_qkv, preferred_element_type=jnp.float32),
        "tensor",
    )
    norm_one_pull = jax.vjp(layer_norm, inputs, gain_one, shift_one)[1]
    grad_in_norm, grad_gain_one, grad_shift_one = norm_one_pull(grad_normed)
    grad_tokens = (grad_middle + grad_in_norm).astype(jnp.bfloat16)
    (
        qkv_part,
        out_part,
        up_part,
        down_part,
        gain_one_part,
        shift_one_part,
        gain_two_part,
        shift_two_part,
    ) = (
        lax.psum_scatter(grad_qkv_local, "dp", scatter_dimension=1, tiled=True),
        lax.psum_scatter(grad_out_local, "dp", scatter_dimension=1, tiled=True),
        lax.psum_scatter(grad_up_local, "dp", scatter_dimension=0, tiled=True),
        lax.psum_scatter(grad_down_local, "dp", scatter_dimension=1, tiled=True),
        lax.psum_scatter(grad_gain_one, "dp", scatter_dimension=0, tiled=True),
        lax.psum_scatter(grad_shift_one, "dp", scatter_dimension=0, tiled=True),
        lax.psum_scatter(grad_gain_two, "dp", scatter_dimension=0, tiled=True),
        lax.psum_scatter(grad_shift_two, "dp", scatter_dimension=0, tiled=True),
    )
    return (
        output,
        grad_tokens,
        qkv_part,
        out_part,
        up_part,
        down_part,
        gain_one_part,
        shift_one_part,
        gain_two_part,
        shift_two_part,
    )


def solution(mesh):
    in_specs = (
        P("dp", None, None),
        P("dp", None, None),
        P("dp"),
        P(None, None, "tensor"),
        P("tensor", None),
        P(None, "tensor"),
        P("tensor", None),
        P(),
        P(),
        P(),
        P(),
    )
    out_specs = (
        P("dp", None, None),
        P("dp", None, None),
        P(None, "dp", "tensor"),
        P("tensor", "dp"),
        P("dp", "tensor"),
        P("tensor", "dp"),
        P("dp"),
        P("dp"),
        P("dp"),
        P("dp"),
    )
    return jax.shard_map(
        per_device, mesh=mesh, in_specs=in_specs, out_specs=out_specs, check_vma=False
    )
```

profile of v0, /device:TPU:0, one launch (start us, length us, event | category | flops | bytes accessed | tf_op | source)
XLA Modules:
  0.0 753.6 jit_solution(12247592497835204554)
XLA Ops:
  8.2 2.3 convert_reduce_fusion
  10.4 2.6 fusion.10
  13.4 2.8 convert_bitcast_fusion
  17.6 1.6 copy.57
  19.2 2.3 copy.56
  22.8 2.9 fusion.4
  25.7 1.7 exponential_reduce_fusion
  27.5 2.3 convolution_convert_fusion.1
  30.7 3.0 fusion.36
  34.0 99.2 %all-reduce.10.cloned.1.call-done = f32[6,260,768]{2,1,0:T(8,128)} async-done(((f32[6,260,768]{2,1,0:T(8,128)}), f32[6,260,768]{2,1,0:T(8,128)}) %all-reduce.10.cloned.1.call-update) | async-done | bytes 4792336 | tf_op jit(solution)/shard_map/psum | solution.py:74
  133.2 3.7 fusion.47
  137.8 3.8 fusion.23
  141.5 11.6 %multiply_convert_fusion.1 = (bf16[6,260,768]{2,1,0:T(8,128)(2,1)}, f32[6,260,768]{2,1,0:T(8,128)S(1)}) fusion(f32[6,260,768]{2,1,0:T(8,128)S(1)} %get-tuple-element.66, u8[260,768]{1,0:T(8,128)(4,1)S(1)} %get-tuple-element.48, u8[260,768]{1,0:T(8,128)(4,1)S(1)} %get-tuple-element.47), kind=kLoop, calls=%fused_computation.35 | loop fusion | flops 83865600 | bytes 12380160 | tf_op jit(solution)/shard_map/convert_element_type | solution.py:46
  153.2 3.4 add_convert_fusion.1
  158.0 4.3 fusion.27
  162.6 96.5 %all-reduce.12.cloned.1.call-done = f32[6,260,768]{2,1,0:T(8,128)} async-done(((f32[6,260,768]{2,1,0:T(8,128)}), f32[6,260,768]{2,1,0:T(8,128)}) %all-reduce.12.cloned.1.call-update) | async-done | bytes 4792336 | tf_op jit(solution)/shard_map/psum | solution.py:93
  259.1 4.9 multiply_reduce_fusion.1
  264.4 3.6 fusion.45
  268.6 1.5 copy-done.7
  271.6 2.4 convolution_bitcast_fusion.4
  274.0 2.5 convolution_convert_fusion.2
  277.8 6.5 convolution_convert_fusion
  284.3 6.8 multiply_reduce_fusion
  291.5 6.3 multiply_convert_fusion
  297.8 1.8 copy-done.6
  299.6 1.9 multiply_convert_fusion.3
  301.5 2.3 copy.66
  303.8 2.2 copy.64
  306.0 3.6 multiply_convert_fusion.2
  310.1 5.0 convolution_bitcast_fusion.3
  315.1 2.8 copy.77
  317.9 4.7 reshape.158
  322.7 6.1 fusion.25
  328.9 4.5 convolution_bitcast_fusion
  333.6 7.4 convolution_bitcast_fusion.2
  341.1 6.2 convolution_bitcast_fusion.1
  348.6 5.2 reduce-scatter.15.cloned.1.call-done
  353.8 1.6 copy.80
  355.5 68.6 %reduce-scatter.13.cloned.1.call-done = f32[96,576]{1,0:T(8,128)} async-done(((f32[768,576]{1,0:T(8,128)}), f32[96,576]{1,0:T(8,128)}) %reduce-scatter.13.cloned.1.call-update) | async-done | bytes 221200
  425.9 174.9 %all-reduce.14.cloned.1.call-done = (f32[6,260,768]{2,1,0:T(8,128)}, f32[6,260,768]{2,1,0:T(8,128)}) async-done(((f32[6,260,768]{2,1,0:T(8,128)}, f32[6,260,768]{2,1,0:T(8,128)}), (f32[6,260,768]{2,1,0:T(8,128)}, f32[6,260,768]{2,1,0:T(8,128)})) %all-reduce.14.cloned.1.call-update) | async-done | bytes 9584656 | tf_op jit(solution)/shard_map/psum | solution.py:77
  600.8 4.6 fusion.44
  605.4 3.9 fusion.9
  609.2 37.2 %all-reduce.4 = (f32[768]{0:T(1024)S(1)}, f32[768]{0:T(1024)S(1)}, f32[768]{0:T(1024)S(1)}, f32[768]{0:T(1024)S(1)}) all-reduce(f32[768]{0:T(1024)S(1)} %get-tuple-element.42, f32[768]{0:T(1024)S(1)} %get-tuple-element.45, f32[768]{0:T(1024)S(1)} %get-tuple-element.40, ...), channel_id=6, replica_groups=mesh['dp'=8,'tensor'=4] {'dp'}, use_global_device_ids=true, to_apply=%region_20.21.clone | all-reduce | flops 3072 | bytes 24576
  648.8 6.0 add_convert_fusion.2
  655.3 1.6 copy-done.9
  656.9 5.0 add_convert_fusion
  661.9 12.3 %reduce-scatter.9.cloned.1.call-done = f32[96,768]{1,0:T(8,128)} async-done(((f32[768,768]{1,0:T(8,128)}), f32[96,768]{1,0:T(8,128)}) %reduce-scatter.9.cloned.1.call-update) | async-done | bytes 294928 | tf_op jit(solution)/shard_map/reduce_scatter | solution.py:146
  674.2 72.4 %reduce-scatter.11.cloned.1.call-done = f32[768,96]{0,1:T(8,128)} async-done(((f32[768,768]{0,1:T(8,128)}), f32[768,96]{0,1:T(8,128)}) %reduce-scatter.11.cloned.1.call-update) | async-done | bytes 294928 | tf_op jit(solution)/shard_map/reduce_scatter | solution.py:147
  (112 shorter events, 18.1 us)
Async XLA Ops:
  7.2 130.5 %copy-start = (bf16[768,768]{1,0:T(8,128)(2,1)S(1)}, bf16[768,768]{1,0:T(8,128)(2,1)}, u32[]{:S(2)}) copy-start(bf16[768,768]{1,0:T(8,128)(2,1)} %param.16) | copy-start | bytes 3538948
  7.2 6.2 copy-start.25
  7.2 6.2 copy-start.31
  7.2 6.2 copy-start.29
  7.2 126.0 %all-reduce.10.cloned.1.call-start = ((), (), s32[]{:S(2)}) async-start(), calls=%async_computation.4 | async-start | bytes 9732096 | tf_op jit(solution)/shard_map/psum | solution.py:74
  7.3 6.1 copy-start.4
  25.7 4.1 copy-start.3
  25.7 1.8 copy-start.14
  27.5 3.2 copy-start.24
  29.8 0.9 copy-start.18
  33.8 225.3 %all-reduce.12.cloned.1.call-start = ((), (), s32[]{:S(2)}) async-start(), calls=%async_computation.5 | async-start | bytes 9732096 | tf_op jit(solution)/shard_map/psum | solution.py:93
  137.0 4.6 copy-start.2
  137.0 0.8 copy-start.26
  137.0 0.8 copy-start.32
  141.5 11.7 %copy-start.11 = (bf16[6,260,768]{2,1,0:T(8,128)(2,1)S(1)}, bf16[6,260,768]{2,1,0:T(8,128)(2,1)}, u32[]{:S(2)}) copy-start(bf16[6,260,768]{2,1,0:T(8,128)(2,1)} %param.12) | copy-start | bytes 7188484
  141.5 11.6 %copy-start.27 = (bf16[768,768]{1,0:T(8,128)(2,1)S(1)}, bf16[768,768]{1,0:T(8,128)(2,1)}, u32[]{:S(2)}) copy-start(bf16[768,768]{1,0:T(8,128)(2,1)} %param.17) | copy-start | bytes 3538948
  156.6 1.4 copy-start.34
  162.3 191.5 %reduce-scatter.15.cloned.1.call-start = ((), (), s32[]{:S(2)}) async-start(), calls=%async_computation.9 | async-start | bytes 884736
  259.1 5.2 copy-start.10
  264.4 3.6 copy-start.12
  268.0 2.2 copy-start.7
  268.0 3.6 copy-start.19
  270.2 1.4 copy-start.17
  277.8 6.5 copy-start.15
  277.8 6.5 copy-start.16
  291.1 132.9 %reduce-scatter.13.cloned.1.call-start = ((), (), s32[]{:S(2)}) async-start(), calls=%async_computation.8 | async-start | bytes 2211840
  297.8 1.8 copy-start.6
  299.6 6.4 copy-start.13
  310.1 5.0 copy-start.22
  317.9 4.8 copy-start.28
  322.6 278.1 %all-reduce.14.cloned.1.call-start = ((), (), s32[]{:S(2)}) async-start(), calls=%async_computation.10 | async-start | bytes 19464192 | tf_op jit(solution)/shard_map/psum | solution.py:77
  322.7 6.1 copy-start.20
  322.7 6.1 copy-start.21
  322.7 6.1 copy-start.23
  322.7 6.1 copy-start.30
  333.4 340.8 %reduce-scatter.9.cloned.1.call-start = ((), (), s32[]{:S(2)}) async-start(), calls=%async_computation.6 | async-start | bytes 2654208 | tf_op jit(solution)/shard_map/reduce_scatter | solution.py:146
  341.1 6.3 copy-start.33
  341.1 405.4 %reduce-scatter.11.cloned.1.call-start = ((), (), s32[]{:S(2)}) async-start(), calls=%async_computation.7 | async-start | bytes 2654208 | tf_op jit(solution)/shard_map/reduce_scatter | solution.py:147
  600.8 4.6 copy-start.8
  605.4 49.4 %slice-start = ((s8[4866048]{0:T(1024)(128)(4,1)}), s8[671744]{0:T(1024)(128)(4,1)S(1)}, s32[]{:S(2)}) async-start(s8[4866048]{0:T(1024)(128)(4,1)} %bitcast.87), calls=%async_computation.11 | async-start | bytes 1343488
  648.8 6.0 copy-start.5
  648.8 6.5 slice-start.1
  648.8 8.1 %copy-start.9 = (f32[6,260,768]{2,1,0:T(8,128)S(1)}, f32[6,260,768]{2,1,0:T(8,128)}, u32[]{:S(2)}) copy-start(f32[6,260,768]{2,1,0:T(8,128)} %get-tuple-element.54) | copy-start | bytes 14376964
  648.8 97.8 %copy-start.1 = (bf16[768,768]{1,0:T(8,128)(2,1)S(1)}, bf16[768,768]{1,0:T(8,128)(2,1)}, u32[]{:S(2)}) copy-start(bf16[768,768]{1,0:T(8,128)(2,1)} %param.16) | copy-start | bytes 3538948
Sparse Core Ops, SparseCore 0:
  33.9 99.2 all-reduce.9
  162.5 96.6 all-reduce.11
  291.2 62.5 reduce-scatter.14
  358.1 65.8 reduce-scatter.12
  426.5 174.2 all-reduce.13
  605.1 69.0 reduce-scatter.8
  678.6 67.8 reduce-scatter.10
where the time goes:
time: 762 us; the launch traced here: 754 us
  waiting for transfers between devices  529 us (69%)
  matrix products  75.3 us (10%)
  other arithmetic  58.8 us (8%)
  blocking collectives  37.2 us (5%)
  local copies, waits for them, and re-layouts  36.4 us (5%)
  between operations  15.5 us (2%)
    psum x1, waiting for transfers between devices, per_device(): output = (middle + lax.psum(branch, 'tensor')).astype(jnp.bfloat16)  175 us
    psum x1, waiting for transfers between devices, per_device(): middle = inputs + lax.psum(partial_out, 'tensor')  99.2 us
    psum x1, waiting for transfers between devices, per_device(): lax.psum(jnp.einsum('btf,df->btd', grad_pre, w_up, preferred_element_type...  96.5 us
    unnamed x9, waiting for transfers between devices  73.9 us
    reduce_scatter x1, waiting for transfers between devices, per_device(): lax.psum_scatter(grad_down_local, 'dp', scatter_dimension=1, tiled=True)  72.4 us
    unnamed x1, blocking collectives  37.2 us
    unnamed x84, local copies, waits for them, and re-layouts  23.5 us
  transfers between devices with their start and end apart: 7, of which 7 were waited for; matrix products, arithmetic and copies ran while one was open for 11% of the time, Pallas kernels for 0%

commit v1 on v0

--- a/solution.py
+++ b/solution.py
@@ -90,9 +90,9 @@
     grad_up_local = jnp.einsum(
         "btd,btf->df", normed_two, grad_pre, preferred_element_type=jnp.float32
     )
-    grad_normed_two = lax.psum(
-        jnp.einsum("btf,df->btd", grad_pre, w_up, preferred_element_type=jnp.float32), "tensor"
-    )
+    part = jnp.einsum("btf,df->btd", grad_pre, w_up, preferred_element_type=jnp.float32)
+    blocks = lax.all_gather(part, "tensor", axis=0, tiled=False)
+    grad_normed_two = blocks.sum(axis=0)
     norm_two_pull = jax.vjp(layer_norm, middle, gain_two, shift_two)[1]
     grad_mid_norm, grad_gain_two, grad_shift_two = norm_two_pull(grad_normed_two)
     grad_middle = grad_output + grad_mid_norm

time: 762 us -> 798 us (1.047)
  waiting for transfers between devices: 529 us -> 547 us
  other arithmetic: 58.8 us -> 76.2 us
    all_gather x0 -> x1, waiting for transfers between devices: none -> 123 us  [per_device(): blocks = lax.all_gather(part, 'tensor', axis=0, tiled=False)]
    psum x1 -> x0, waiting for transfers between devices: 96.5 us -> none  [per_device(): lax.psum(jnp.einsum('btf,df->btd', grad_pre, w_up, preferred_element_type...]
    reduce_sum x0 -> x1, other arithmetic: none -> 9.89 us  [per_device(): grad_normed_two = blocks.sum(axis=0)]
    unnamed x9, waiting for transfers between devices: 73.9 us -> 65.5 us
    reduce_sum x3 -> x4, other arithmetic: 13.4 us -> 20.9 us  [layer_norm(): return centered * lax.rsqrt(variance + EPSILON) * gain_vec + shift_vec]
  transfers between devices with their start and end apart: 7 -> 7, of which waited for: 7 -> 6; matrix products, arithmetic and copies ran while one was open for 11% -> 11% of each run, Pallas kernels for 0% -> 0%
where the time goes in v1:
time: 798 us; the launch traced here: 789 us
  waiting for transfers between devices  547 us (69%)
  other arithmetic  76.2 us (10%)
  matrix products  75.4 us (9%)
  blocking collectives  37.3 us (5%)
  local copies, waits for them, and re-layouts  36.5 us (5%)
  between operations  15.5 us (2%)
    psum x1, waiting for transfers between devices, per_device(): output = (middle + lax.psum(branch, 'tensor')).astype(jnp.bfloat16)  175 us
    all_gather x1, waiting for transfers between devices, per_device(): blocks = lax.all_gather(part, 'tensor', axis=0, tiled=False)  123 us
    psum x1, waiting for transfers between devices, per_device(): middle = inputs + lax.psum(partial_out, 'tensor')  99.2 us
    reduce_scatter x1, waiting for transfers between devices, per_device(): lax.psum_scatter(grad_down_local, 'dp', scatter_dimension=1, tiled=True)  72.3 us
    unnamed x9, waiting for transfers between devices  65.5 us
    unnamed x1, blocking collectives  37.3 us
    unnamed x84, local copies, waits for them, and re-layouts  23.8 us
    reduce_sum x4, other arithmetic, layer_norm(): return centered * lax.rsqrt(variance + EPSILON) * gain_vec + shift_vec  20.9 us
  transfers between devices with their start and end apart: 7, of which 6 were waited for; matrix products, arithmetic and copies ran while one was open for 11% of the time, Pallas kernels for 0%

profile of v1, /device:TPU:0, one launch (start us, length us, event | category | flops | bytes accessed | tf_op | source)
XLA Modules:
  0.0 789.4 jit_solution(2074817578457741909)
XLA Ops:
  8.2 2.3 convert_reduce_fusion
  10.4 2.6 fusion.10
  13.4 2.8 convert_bitcast_fusion
  17.6 1.6 copy.57
  19.2 2.2 copy.56
  22.7 2.9 fusion.4
  25.6 1.7 exponential_reduce_fusion
  27.4 2.3 convolution_convert_fusion.1
  30.7 3.1 fusion.36
  34.0 99.2 %all-reduce.9.cloned.1.call-done = f32[6,260,768]{2,1,0:T(8,128)} async-done(((f32[6,260,768]{2,1,0:T(8,128)}), f32[6,260,768]{2,1,0:T(8,128)}) %all-reduce.9.cloned.1.call-update) | async-done | bytes 4792336 | tf_op jit(solution)/shard_map/psum | solution.py:74
  133.2 3.7 fusion.47
  137.7 3.7 fusion.23
  141.5 11.6 %multiply_convert_fusion.1 = (bf16[6,260,768]{2,1,0:T(8,128)(2,1)}, f32[6,260,768]{2,1,0:T(8,128)S(1)}) fusion(f32[6,260,768]{2,1,0:T(8,128)S(1)} %get-tuple-element.65, u8[260,768]{1,0:T(8,128)(4,1)S(1)} %get-tuple-element.47, u8[260,768]{1,0:T(8,128)(4,1)S(1)} %get-tuple-element.46), kind=kLoop, calls=%fused_computation.35 | loop fusion | flops 83865600 | bytes 12380160 | tf_op jit(solution)/shard_map/convert_element_type | solution.py:46
  153.2 3.4 add_convert_fusion.1
  158.0 4.4 fusion.27
  162.7 123.2 %all-gather.3.cloned.1.call-done = f32[24,260,768]{2,1,0:T(8,128)} async-done(((f32[6,260,768]{2,1,0:T(8,128)}), f32[24,260,768]{2,1,0:T(8,128)}) %all-gather.3.cloned.1.call-update) | async-done | bytes 19169296 | tf_op jit(solution)/shard_map/all_gather | solution.py:94
  285.9 9.9 %reduce_sum.140 = f32[6,260,768]{2,1,0:T(8,128)} reduce(f32[4,6,260,768]{3,2,1,0:T(8,128)} %bitcast.88, f32[]{:T(128)} %constant.38.clone.1), dimensions={0}, to_apply=%region_8.9 | reduce | flops 3594240 | bytes 23961604 | tf_op jit(solution)/shard_map/reduce_sum | solution.py:95
  295.8 4.8 multiply_reduce_fusion.1
  301.0 3.6 fusion.45
  308.2 2.4 convolution_bitcast_fusion.4
  310.6 2.5 convolution_convert_fusion.2
  314.4 6.5 convolution_convert_fusion
  320.9 6.7 multiply_reduce_fusion
  328.1 6.3 multiply_convert_fusion
  334.4 1.8 copy-done.6
  336.2 1.9 multiply_convert_fusion.3
  338.1 2.2 copy.66
  340.3 2.2 copy.64
  342.5 3.5 multiply_convert_fusion.2
  346.7 5.0 convolution_bitcast_fusion.3
  351.7 2.8 copy.77
  354.5 4.8 reshape.159
  359.4 6.1 fusion.25
  365.5 4.6 convolution_bitcast_fusion
  370.3 7.4 convolution_bitcast_fusion.2
  377.8 6.2 convolution_bitcast_fusion.1
  385.4 7.6 reduce_sum.155
  393.0 1.6 copy.80
  394.6 65.3 %reduce-scatter.13.cloned.1.call-done = f32[96,576]{1,0:T(8,128)} async-done(((f32[768,576]{1,0:T(8,128)}), f32[96,576]{1,0:T(8,128)}) %reduce-scatter.13.cloned.1.call-update) | async-done | bytes 221200
  461.9 175.1 %all-reduce.11.cloned.1.call-done = (f32[6,260,768]{2,1,0:T(8,128)}, f32[6,260,768]{2,1,0:T(8,128)}) async-done(((f32[6,260,768]{2,1,0:T(8,128)}, f32[6,260,768]{2,1,0:T(8,128)}), (f32[6,260,768]{2,1,0:T(8,128)}, f32[6,260,768]{2,1,0:T(8,128)})) %all-reduce.11.cloned.1.call-update) | async-done | bytes 9584656 | tf_op jit(solution)/shard_map/psum | solution.py:77
  636.9 4.6 fusion.44
  641.5 3.8 fusion.9
  645.4 37.3 %all-reduce.4 = (f32[768]{0:T(1024)S(1)}, f32[768]{0:T(1024)S(1)}, f32[768]{0:T(1024)S(1)}, f32[768]{0:T(1024)S(1)}) all-reduce(f32[768]{0:T(1024)S(1)} %get-tuple-element.42, f32[768]{0:T(1024)S(1)} %get-tuple-element.44, f32[768]{0:T(1024)S(1)} %get-tuple-element.40, ...), channel_id=7, replica_groups=mesh['dp'=8,'tensor'=4] {'dp'}, use_global_device_ids=true, to_apply=%region_20.21.clone | all-reduce | flops 3072 | bytes 24576
  685.1 6.0 add_convert_fusion.2
  691.6 1.6 copy-done.9
  693.2 5.0 add_convert_fusion
  698.2 12.0 %reduce-scatter.9.cloned.1.call-done = f32[96,768]{1,0:T(8,128)} async-done(((f32[768,768]{1,0:T(8,128)}), f32[96,768]{1,0:T(8,128)}) %reduce-scatter.9.cloned.1.call-update) | async-done | bytes 294928 | tf_op jit(solution)/shard_map/reduce_scatter | solution.py:146
  710.1 72.3 %reduce-scatter.11.cloned.1.call-done = f32[768,96]{0,1:T(8,128)} async-done(((f32[768,768]{0,1:T(8,128)}), f32[768,96]{0,1:T(8,128)}) %reduce-scatter.11.cloned.1.call-update) | async-done | bytes 294928 | tf_op jit(solution)/shard_map/reduce_scatter | solution.py:147
  (114 shorter events, 19.6 us)
Async XLA Ops:
  7.2 130.5 %copy-start = (bf16[768,768]{1,0:T(8,128)(2,1)S(1)}, bf16[768,768]{1,0:T(8,128)(2,1)}, u32[]{:S(2)}) copy-start(bf16[768,768]{1,0:T(8,128)(2,1)} %param.16) | copy-start | bytes 3538948
  7.2 6.2 copy-start.25
  7.2 6.2 copy-start.31
  7.2 6.2 copy-start.29
  7.2 126.0 %all-reduce.9.cloned.1.call-start = ((), (), s32[]{:S(2)}) async-start(), calls=%async_computation.4 | async-start | bytes 9732096 | tf_op jit(solution)/shard_map/psum | solution.py:74
  7.3 6.1 copy-start.4
  25.6 4.1 copy-start.3
  25.6 1.8 copy-start.14
  27.4 3.2 copy-start.24
  29.7 0.9 copy-start.18
  33.8 252.1 %all-gather.3.cloned.1.call-start = ((), (), s32[]{:S(2)}) async-start(), calls=%async_computation.7 | async-start | bytes 24330240 | tf_op jit(solution)/shard_map/all_gather | solution.py:94
  136.9 4.5 copy-start.2
  136.9 0.8 copy-start.26
  137.0 0.8 copy-start.32
  141.5 11.7 %copy-start.11 = (bf16[6,260,768]{2,1,0:T(8,128)(2,1)S(1)}, bf16[6,260,768]{2,1,0:T(8,128)(2,1)}, u32[]{:S(2)}) copy-start(bf16[6,260,768]{2,1,0:T(8,128)(2,1)} %param.12) | copy-start | bytes 7188484
  141.5 11.6 %copy-start.27 = (bf16[768,768]{1,0:T(8,128)(2,1)S(1)}, bf16[768,768]{1,0:T(8,128)(2,1)}, u32[]{:S(2)}) copy-start(bf16[768,768]{1,0:T(8,128)(2,1)} %param.17) | copy-start | bytes 3538948
  156.5 1.5 copy-start.34
  162.4 230.6 %reduce-scatter.15.cloned.1.call-start = ((), (), s32[]{:S(2)}) async-start(), calls=%async_computation.9 | async-start | bytes 884736
  295.8 5.2 copy-start.10
  301.0 3.6 copy-start.12
  304.6 2.2 copy-start.7
  304.6 3.6 copy-start.19
  306.8 1.4 copy-start.17
  314.4 6.5 copy-start.15
  314.4 6.5 copy-start.16
  327.6 132.3 %reduce-scatter.13.cloned.1.call-start = ((), (), s32[]{:S(2)}) async-start(), calls=%async_computation.8 | async-start | bytes 2211840
  334.4 1.9 copy-start.6
  336.2 6.3 copy-start.13
  346.7 5.0 copy-start.22
  354.5 4.8 copy-start.28
  359.3 277.7 %all-reduce.11.cloned.1.call-start = ((), (), s32[]{:S(2)}) async-start(), calls=%async_computation.10 | async-start | bytes 19464192 | tf_op jit(solution)/shard_map/psum | solution.py:77
  359.3 6.2 copy-start.20
  359.3 6.2 copy-start.21
  359.3 6.2 copy-start.23
  359.4 6.1 copy-start.30
  370.1 340.0 %reduce-scatter.9.cloned.1.call-start = ((), (), s32[]{:S(2)}) async-start(), calls=%async_computation.5 | async-start | bytes 2654208 | tf_op jit(solution)/shard_map/reduce_scatter | solution.py:146
  377.8 6.3 copy-start.33
  377.8 404.6 %reduce-scatter.11.cloned.1.call-start = ((), (), s32[]{:S(2)}) async-start(), calls=%async_computation.6 | async-start | bytes 2654208 | tf_op jit(solution)/shard_map/reduce_scatter | solution.py:147
  636.9 4.6 copy-start.8
  641.5 49.5 %slice-start = ((s8[4866048]{0:T(1024)(128)(4,1)}), s8[671744]{0:T(1024)(128)(4,1)S(1)}, s32[]{:S(2)}) async-start(s8[4866048]{0:T(1024)(128)(4,1)} %bitcast.89), calls=%async_computation.11 | async-start | bytes 1343488
  685.1 6.0 copy-start.5
  685.1 6.5 slice-start.1
  685.1 8.1 %copy-start.9 = (f32[6,260,768]{2,1,0:T(8,128)S(1)}, f32[6,260,768]{2,1,0:T(8,128)}, u32[]{:S(2)}) copy-start(f32[6,260,768]{2,1,0:T(8,128)} %get-tuple-element.53) | copy-start | bytes 14376964
  685.1 97.3 %copy-start.1 = (bf16[768,768]{1,0:T(8,128)(2,1)S(1)}, bf16[768,768]{1,0:T(8,128)(2,1)}, u32[]{:S(2)}) copy-start(bf16[768,768]{1,0:T(8,128)(2,1)} %param.16) | copy-start | bytes 3538948
Sparse Core Ops, SparseCore 0:
  33.9 99.2 all-reduce.8
  162.5 123.3 all-gather.2
  327.7 62.4 reduce-scatter.14
  394.2 65.7 reduce-scatter.12
  462.6 174.2 all-reduce.10
  640.8 69.2 reduce-scatter.8
  714.2 68.1 reduce-scatter.10
